TPU v7x, 512 devices: a whole 4x4x16 slice. The times are simulated.
512 devices in a mesh: leaf: 128 (over x_hi, z, y), sub: 4 (over x_lo, core).
Axes of the slice: x: 4 (x_hi: 2, x_lo: 2; x = x_hi * 2 + x_lo), y: 4, z: 16, core: 2. Of those that a mesh axis runs over, the one named last changes fastest.
Arguments:
- points: float32 [16384, 3, 128], P(('leaf', 'sub')), may hold values from 0 to 1
- charges: float32 [16384, 8, 128], P(('leaf', 'sub')), may hold values from -6 to 6
- leaf_skel: float32 [16384, 3, 64], P(('leaf', 'sub')), may hold values from 0 to 1
- mid_skel: float32 [2048, 3, 64], P(('leaf', 'sub')), may hold values from 0 to 1
- root_skel: float32 [128, 3, 64], replicated, may hold values from 0 to 1
- leaf_transfer: float32 [16384, 64, 64], P(('leaf', 'sub')), may hold values from -0.25 to 0.25
- mid_transfer: float32 [2048, 64, 64], P(('leaf', 'sub')), may hold values from -0.75 to 0.75
- near_list: int32 [16384, 27], P(('leaf', 'sub')), may hold values from -1 to 16383, as said below
- far_list: int32 [16384, 20], P(('leaf', 'sub')), may hold values from -1 to 16383, as said below
- mid_list: int32 [2048, 6], P(('leaf', 'sub')), may hold values from -1 to 2047, as said below
- root_list: int32 [128, 6], P('leaf'), may hold values from -1 to 127, as said below
Outputs:
- potentials: float32 [16384, 8, 128], P(('leaf', 'sub'))
Inputs may be any that keep to these rules, and one draw needn't show every extreme that they name: `near_list`: slot 0 of a leaf's row is the leaf itself. Every other entry is -1 or a leaf other than itself that lies on the same device or on one of the two devices beside it in the order of leaf indices; no leaf appears twice in the near and coupling rows of one leaf together. `far_list`: every entry is -1 or a leaf other than the row's own that lies on the same device or on one of the two devices beside it in the order of leaf indices, never one of the row's near_list entries. `mid_list`: every entry is -1 or a middle cluster other than the row's own under the same subtree root, at most once in a row. `root_list`: every entry is -1 or a root other than the row's own, at most once in a row.
All inputs are finite; a program needn't handle non-finite values.
Results may differ from a plain program's by a relative error of at most 0.0003.
Values sent between devices are 32-bit elements; how exact they have to be, the bound alone decides.
A program may use at most 64 MiB of HBM per device.

v0:
```python
import math
import jax
import jax.numpy as jnp
from jax import lax
from jax.sharding import PartitionSpec as P

DELTA2 = 0.0025
EXACT_PRECISION = lax.Precision.HIGHEST


def extended(block, sides, width):
    for axis, dim in sides:
        count = lax.axis_size(axis)
        forward = [(i, i + 1) for i in range(count - 1)]
        backward = [(target, source) for source, target in forward]
        low = lax.ppermute(
            lax.slice_in_dim(block, block.shape[dim] - width, None, axis=dim), axis, forward
        )
        high = lax.ppermute(lax.slice_in_dim(block, 0, width, axis=dim), axis, backward)
        block = jnp.concatenate([low, block, high], axis=dim)
    return block


def kernel(targets, sources):
    first = targets[:, 0, :, None] - sources[:, 0, None, :]
    second = targets[:, 1, :, None] - sources[:, 1, None, :]
    third = targets[:, 2, :, None] - sources[:, 2, None, :]
    return 1.0 / jnp.sqrt(first * first + second * second + third * third + DELTA2)


def lookup(table, partner_idx, offset):
    present = (partner_idx >= 0).astype(jnp.float32)
    position = jnp.clip(partner_idx - offset, 0, table.shape[0] - 1)
    return (table[position], present)


def couple(target_skel, coeff_table, skel_table, lists, offset, nrhs_count, scale):

    def add_slot(slot_no, running):
        partner_idx = lax.dynamic_slice_in_dim(lists, slot_no, 1, 1)[:, 0]
        partner_coeffs, present = lookup(coeff_table, partner_idx, offset)
        partner_skel, unused = lookup(skel_table, partner_idx, offset)
        matrix = kernel(target_skel, partner_skel)
        term = jnp.einsum("lab,lrb->lra", matrix, partner_coeffs, precision=EXACT_PRECISION)
        return running + term * (present * scale)[:, None, None]

    start_value = jnp.zeros((target_skel.shape[0], nrhs_count, coeff_table.shape[2]), jnp.float32)
    return lax.fori_loop(0, lists.shape[1], add_slot, start_value)


def local(
    points,
    charges,
    leaf_skel,
    mid_skel,
    root_skel,
    leaf_transfer,
    mid_transfer,
    near_list,
    far_list,
    mid_list,
    root_list,
):
    leaves = points.shape[0]
    nrhs_count = charges.shape[1]
    rank_count = leaf_skel.shape[2]
    leaf_count = points.shape[2]
    leaf_scale = 1.0 / math.sqrt(leaf_count)
    rank_scale = 1.0 / rank_count
    flat_index = lax.axis_index(("leaf", "sub"))
    window_start = (flat_index - 1) * leaves
    packed_points = jnp.concatenate([points, charges], axis=1)
    widened = extended(packed_points, ((("leaf", "sub"), 0),), leaves)

    def add_near(slot_no, running):
        partner_idx = lax.dynamic_slice_in_dim(near_list, slot_no, 1, 1)[:, 0]
        partner_rows, present = lookup(widened, partner_idx, window_start)
        matrix = kernel(points, partner_rows[:, :3])
        term = jnp.einsum("lpq,lrq->lrp", matrix, partner_rows[:, 3:], precision=EXACT_PRECISION)
        return running + term * (present / leaf_count)[:, None, None]

    near = lax.fori_loop(0, near_list.shape[1], add_near, jnp.zeros(charges.shape, jnp.float32))
    basis = kernel(points, leaf_skel)
    expansion_weights = (
        jnp.einsum("lpa,lrp->lra", basis, charges, precision=EXACT_PRECISION) * leaf_scale
    )
    packed_coeffs = jnp.concatenate([expansion_weights, leaf_skel], axis=1)
    fine_table = extended(packed_coeffs, ((("leaf", "sub"), 0),), leaves)
    leaf_potential_field = couple(
        leaf_skel,
        fine_table[:, :nrhs_count],
        fine_table[:, nrhs_count:],
        far_list,
        window_start,
        nrhs_count,
        rank_scale,
    )
    mids = leaves // 8
    leaf_cluster_groups = leaf_transfer.reshape(mids, 8, rank_count, rank_count)
    middle_expansion_weights = jnp.einsum(
        "hpsi,hpds->hdi",
        leaf_cluster_groups,
        expansion_weights.reshape(mids, 8, nrhs_count, rank_count),
        precision=EXACT_PRECISION,
    )
    packed_mid = jnp.concatenate([middle_expansion_weights, mid_skel], axis=1)
    mid_table = lax.all_gather(packed_mid, "sub", axis=0, tiled=True)
    group_start = lax.axis_index("leaf") * mid_table.shape[0]
    mid_field = couple(
        mid_skel,
        mid_table[:, :nrhs_count],
        mid_table[:, nrhs_count:],
        mid_list,
        group_start,
        nrhs_count,
        rank_scale,
    )
    partial_root = jnp.einsum(
        "mab,mra->rb", mid_transfer, middle_expansion_weights, precision=EXACT_PRECISION
    )
    summed_root = lax.psum(partial_root, "sub")
    root_table = lax.all_gather(summed_root[None], "leaf", axis=0, tiled=True)
    root_number = lax.axis_index("leaf")
    my_skel = lax.dynamic_slice_in_dim(root_skel, root_number, 1, 0)
    root_field = couple(my_skel, root_table, root_skel, root_list, 0, nrhs_count, rank_scale)
    middle_potential_total = mid_field + jnp.einsum(
        "mab,rb->mra", mid_transfer, root_field[0], precision=EXACT_PRECISION
    )
    leaf_potential_total = leaf_potential_field + jnp.einsum(
        "oxgc,osc->oxsg", leaf_cluster_groups, middle_potential_total, precision=EXACT_PRECISION
    ).reshape(leaves, nrhs_count, rank_count)
    return (
        near
        + jnp.einsum("lpa,lra->lrp", basis, leaf_potential_total, precision=EXACT_PRECISION)
        * leaf_scale
    )


def solution(mesh):
    in_specs = (
        P(("leaf", "sub"), None, None),
        P(("leaf", "sub"), None, None),
        P(("leaf", "sub"), None, None),
        P(("leaf", "sub"), None, None),
        P(),
        P(("leaf", "sub"), None, None),
        P(("leaf", "sub"), None, None),
        P(("leaf", "sub"), None),
        P(("leaf", "sub"), None),
        P(("leaf", "sub"), None),
        P("leaf", None),
    )
    out_specs = P(("leaf", "sub"), None, None)
    return jax.shard_map(local, mesh=mesh, in_specs=in_specs, out_specs=out_specs, check_vma=False)
```

profile of v0, /device:TPU:2, one launch (start us, length us, event | category | flops | bytes accessed | tf_op | source)
XLA Modules:
  0.0 699.5 jit_solution(9708654243711353516)
XLA Ops:
  13.6 5.6 collective-permute-start.1
  19.9 5.4 all_gather.6
  25.4 10.1 %while.60 = (s32[]{:T(128)}, f32[4,8,64]{2,1,0:T(8,128)S(1)}, s32[4,6]{0,1:T(8,128)S(1)}, s32[]{:T(128)}, f32[16,8,64]{2,1,0:T(8,128)S(1)}, /*index=5*/f32[4,3,6...) while((s32[]{:T(128)}, f32[4,8,64]{2,1,0:T(8,128)S(1)}, s32[4,6]{0,1:T(8,128)S(1)}, ...), condition=%wide.region_5.6_spmd.clone, body=%wide.region_4.5_spmd.clone.sunk | while | flops 1727519 | bytes 69875 | solution.py:48
  35.8 7.4 %psum.7 = f32[1,8,64]{2,1,0:T(8,128)S(1)} all-reduce(f32[1,8,64]{2,1,0:T(8,128)S(1)} %convolution_bitcast_fusion.2), channel_id=1, replica_groups=mesh['leaf'=128,'sub'=4] {'sub'}, use_global_device_ids=true, to_apply=%region_6.7 | all-reduce | flops 512 | bytes 4096 | tf_op jit(solution)/shard_map/psum | solution.py:121
  43.2 364.2 %all_gather.7 = f32[128,8,64]{2,1,0:T(8,128)S(1)} all-gather(f32[1,8,64]{2,1,0:T(8,128)S(1)} %psum.7), channel_id=1, replica_groups=mesh['leaf'=128,'sub'=4] {'leaf'}, dimensions={0}, use_global_device_ids=true | all-gather | bytes 264192 | tf_op jit(solution)/shard_map/all_gather | solution.py:122
  407.6 12.6 %while.61 = (s32[]{:T(128)}, f32[1,8,64]{2,1,0:T(8,128)S(1)}, s32[1,6]{1,0:T(1,128)S(1)}, f32[128,8,64]{2,1,0:T(8,128)S(1)}, f32[1,3,64]{2,1,0:T(4,128)S(1)}, /*...) while((s32[]{:T(128)}, f32[1,8,64]{2,1,0:T(8,128)S(1)}, ...), condition=%wide.region_8.9_spmd.clone, body=%wide.region_7.8_spmd.clone.sunk | while | flops 431623 | bytes 18109 | solution.py:48
  425.1 113.0 %while.59 = (s32[]{:T(128)}, f32[32,8,64]{2,1,0:T(8,128)S(1)}, s32[32,20]{0,1:T(8,128)}, s32[]{:T(128)}, f32[96,8,64]{2,1,0:T(8,128)S(1)}, /*index=5*/f32[32,3,6...) while((s32[]{:T(128)}, f32[32,8,64]{2,1,0:T(8,128)S(1)}, s32[32,20]{0,1:T(8,128)}, ...), condition=%wide.region_3.4_spmd.clone, body=%wide.region_2.3_spmd.clone.sunk | while | flops 13812963 | bytes 529523 | solution.py:48
  541.2 157.6 %while.58 = (s32[]{:T(128)}, f32[32,8,128]{2,1,0:T(8,128)S(1)}, s32[32,27]{0,1:T(8,128)S(1)}, s32[]{:T(128)}, f32[96,11,128]{2,1,0:T(8,128)S(1)}, /*index=5*/f32[32,3,128]{2,0,1:T(8,128)S(1)}, s32[]{:T(128)}, s32[]{:T(128)}) while((s32[]{:T(128)}, f32[32,8,128]{2,1,0:T(8,128)S(1)}, s32[32,27]{0,1:T(8,128)S(1)}, s32[]{:T(128)}, ...), condition=%wide.region_1.2_spmd.clone, body=%wide.region_0.1_spmd.clone.sunk | while | flops 55149792 | bytes 1054059 | solution.py:82
  542.0 5.1 fusion.156
  547.8 5.1 fusion.156
  553.6 5.1 fusion.156
  559.5 5.1 fusion.156
  565.3 5.1 fusion.156
  571.2 5.1 fusion.156
  577.0 5.1 fusion.156
  582.8 5.1 fusion.156
  588.7 5.1 fusion.156
  594.5 5.1 fusion.156
  600.3 5.1 fusion.156
  629.5 5.1 fusion.156
  635.4 5.1 fusion.156
  641.2 5.1 fusion.156
  687.9 5.1 fusion.156
  693.7 5.1 fusion.156
  (479 shorter events, 224.5 us)
Async XLA Ops:
  0.0 19.2 %copy-start = (f32[32,64,64]{2,1,0:T(8,128)S(1)}, f32[32,64,64]{2,1,0:T(8,128)}, u32[]{:S(2)}) copy-start(f32[32,64,64]{2,1,0:T(8,128)} %param.24) | copy-start | bytes 1572868
  2.4 3.5 copy-start.10
  2.4 3.5 copy-start.12
  2.4 9.2 %copy-start.2 = (f32[32,3,128]{2,0,1:T(8,128)S(1)}, f32[32,3,128]{2,0,1:T(8,128)}, u32[]{:S(2)}) copy-start(f32[32,3,128]{2,0,1:T(8,128)} %param.19) | copy-start | bytes 147460
  2.5 9.2 %copy-start.3 = (f32[32,8,128]{2,1,0:T(8,128)S(1)}, f32[32,8,128]{2,1,0:T(8,128)}, u32[]{:S(2)}) copy-start(f32[32,8,128]{2,1,0:T(8,128)} %param.20) | copy-start | bytes 393220
  2.5 16.7 %copy-start.5 = (f32[4,3,64]{2,0,1:T(4,128)S(1)}, f32[4,3,64]{2,0,1:T(4,128)}, u32[]{:S(2)}) copy-start(f32[4,3,64]{2,0,1:T(4,128)} %param.22) | copy-start | bytes 9220
  6.0 417.5 %collective-permute-start.2 = (f32[32,11,64]{2,1,0:T(8,128)S(1)}, f32[32,11,64]{2,1,0:T(8,128)S(1)}, u32[]{:S(2)}, u32[]{:S(2)}) collective-permute-start(f32[32,11,64]{2,1,0:T(8,128)S(1)} %pad_maximum_fusion.3), channel_id=1, source_target_pairs={{0,1},{1,2},{2,3},{3,4},{4,5},{5,6},{6,7},{7,8},{8,9},{9,10},{10,1... | collective-permute-start | bytes 270344 | tf_op jit(solution)/shard_map/ppermute | solution.py:16
  7.9 415.7 %collective-permute-start.3 = (f32[32,11,64]{2,1,0:T(8,128)S(1)}, f32[32,11,64]{2,1,0:T(8,128)S(1)}, u32[]{:S(2)}, u32[]{:S(2)}) collective-permute-start(f32[32,11,64]{2,1,0:T(8,128)S(1)} %pad_maximum_fusion.3), channel_id=1, source_target_pairs={{1,0},{2,1},{3,2},{4,3},{5,4},{6,5},{7,6},{8,7},{9,8},{10,9},{11,1... | collective-permute-start | bytes 270344 | tf_op jit(solution)/shard_map/ppermute | solution.py:19
  11.7 13.7 %copy-start.15 = (s32[4,6]{1,0:T(4,128)S(1)}, s32[4,6]{1,0:T(4,128)}, u32[]{:S(2)}) copy-start(s32[4,6]{1,0:T(4,128)} %param.28) | copy-start | bytes 292
  11.7 528.4 %collective-permute-start = (f32[32,11,128]{2,1,0:T(8,128)S(1)}, f32[32,11,128]{2,1,0:T(8,128)}, u32[]{:S(2)}, u32[]{:S(2)}) collective-permute-start(f32[32,11,128]{2,1,0:T(8,128)S(1)} %pad_maximum_fusion.2), channel_id=1, source_target_pairs={{0,1},{1,2},{2,3},{3,4},{4,5},{5,6},{6,7},{7,8},{8,9},{9,10},{10,1... | collective-permute-start | bytes 540680 | tf_op jit(solution)/shard_map/ppermute | solution.py:16
  13.6 526.5 %collective-permute-start.1 = (f32[32,11,128]{2,1,0:T(8,128)S(1)}, f32[32,11,128]{2,1,0:T(8,128)}, u32[]{:S(2)}, u32[]{:S(2)}) collective-permute-start(f32[32,11,128]{2,1,0:T(8,128)S(1)} %pad_maximum_fusion.2), channel_id=1, source_target_pairs={{1,0},{2,1},{3,2},{4,3},{5,4},{6,5},{7,6},{8,7},{9,8},{10,9},{11,1... | collective-permute-start | bytes 540680 | tf_op jit(solution)/shard_map/ppermute | solution.py:19
  25.4 10.1 %copy-start.4 = (f32[4,64,64]{2,1,0:T(8,128)S(1)}, f32[4,64,64]{2,1,0:T(8,128)}, u32[]{:S(2)}) copy-start(f32[4,64,64]{2,1,0:T(8,128)} %param.25) | copy-start | bytes 196612
  25.4 382.0 %copy-start.8 = (f32[128,3,64]{0,2,1:T(8,128)S(1)}, f32[128,3,64]{0,2,1:T(8,128)}, u32[]{:S(2)}) copy-start(f32[128,3,64]{0,2,1:T(8,128)} %param.23) | copy-start | bytes 294916
  35.5 372.0 %copy-start.14 = (s32[1,6]{1,0:T(1,128)S(1)}, s32[1,6]{1,0:T(1,128)}, u32[]{:S(2)}) copy-start(s32[1,6]{1,0:T(1,128)} %param.29) | copy-start | bytes 76
  420.2 3.2 copy-start.9
  424.1 0.8 copy-start.1
  424.1 0.9 copy-start.7
  425.1 113.1 %copy-start.11 = (f32[32,128]{1,0:T(8,128)S(1)}, f32[32,128]{1,0:T(8,128)}, u32[]{:S(2)}) copy-start(f32[32,128]{1,0:T(8,128)} %copy-done.10) | copy-start | bytes 49156
  425.1 113.1 %copy-start.13 = (f32[32,128]{1,0:T(8,128)S(1)}, f32[32,128]{1,0:T(8,128)}, u32[]{:S(2)}) copy-start(f32[32,128]{1,0:T(8,128)} %copy-done.12) | copy-start | bytes 49156
  540.1 1.2 copy-start.6
where the time goes:
time: 703 us; the launch traced here: 700 us
  blocking collectives  377 us (54%)
  matrix products  211 us (30%)
  local copies, waits for them, and re-layouts  52.6 us (7%)
  other arithmetic  35.4 us (5%)
  starting transfers between devices  13 us (2%)
  loops' own time  10.1 us (1%)
    all_gather x1, blocking collectives, local(): root_table = lax.all_gather(summed_root[None], 'leaf', axis=0, tiled=True)  364 us
    dot_general x27, matrix products, add_near(): jnp.einsum('lpq,lrq->lrp', matrix, partner_rows[:, 3:], precision=EXACT_P...  138 us
    dot_general x32, matrix products, add_slot(): jnp.einsum('lab,lrb->lra', matrix, partner_coeffs, precision=EXACT_PRECIS...  63.4 us
    gather x85, local copies, waits for them, and re-layouts, lookup(): return (table[position], present)  46.5 us
    select_n x53, other arithmetic, lookup(): return (table[position], present)  14.7 us
  transfers between devices with their start and end apart: 4, of which 0 were waited for; matrix products, arithmetic and copies ran while one was open for 19% of the time, Pallas kernels for 0%

commit v1 on v0

--- a/solution.py
+++ b/solution.py
@@ -119,7 +119,9 @@
         "mab,mra->rb", mid_transfer, middle_expansion_weights, precision=EXACT_PRECISION
     )
     summed_root = lax.psum(partial_root, "sub")
-    root_table = lax.all_gather(summed_root[None], "leaf", axis=0, tiled=True)
+    root_table = jnp.concatenate(
+        lax.all_to_all(jnp.stack([summed_root[None]] * lax.axis_size("leaf")), "leaf", 0, 0), axis=0
+    )
     root_number = lax.axis_index("leaf")
     my_skel = lax.dynamic_slice_in_dim(root_skel, root_number, 1, 0)
     root_field = couple(my_skel, root_table, root_skel, root_list, 0, nrhs_count, rank_scale)

time: 703 us -> 408 us (0.58)
  the two profiles are of different devices: /device:TPU:2 before, /device:TPU:1 now
where the time goes in v1:
time: 408 us; the launch traced here: 405 us
  matrix products  248 us (61%)
  local copies, waits for them, and re-layouts  57.6 us (14%)
  starting transfers between devices  40.6 us (10%)
  other arithmetic  36.7 us (9%)
  blocking collectives  11.5 us (3%)
  loops' own time  10.1 us (2%)
    dot_general x27, matrix products, add_near(): jnp.einsum('lpq,lrq->lrp', matrix, partner_rows[:, 3:], precision=EXACT_P...  175 us
    dot_general x32, matrix products, add_slot(): jnp.einsum('lab,lrb->lra', matrix, partner_coeffs, precision=EXACT_PRECIS...  63.4 us
    gather x85, local copies, waits for them, and re-layouts, lookup(): return (table[position], present)  46.4 us
    all_to_all x1, starting transfers between devices, local(): lax.all_to_all(jnp.stack([summed_root[None]] * lax.axis_size('leaf')), 'l...  24.7 us
    select_n x53, other arithmetic, lookup(): return (table[position], present)  14.4 us
    mul x26, other arithmetic, add_slot(): return running + term * (present * scale)[:, None, None]  14 us
    ppermute x2, starting transfers between devices, extended(): lax.ppermute(lax.slice_in_dim(block, 0, width, axis=dim), axis, backward)  9.33 us
    another operation x3, loops' own time, couple(): return lax.fori_loop(0, lists.shape[1], add_slot, start_value)  8.88 us
  transfers between devices with their start and end apart: 5, of which 0 were waited for; matrix products, arithmetic and copies ran while one was open for 79% of the time, Pallas kernels for 0%

profile of v1, /device:TPU:1, one launch (start us, length us, event | category | flops | bytes accessed | tf_op | source)
XLA Modules:
  0.0 404.8 jit_solution(1170732939094853930)
XLA Ops:
  29.1 24.7 %all-to-all-start = ((f32[128,1,512]{2,1,0:T(1,128)}), f32[128,1,512]{2,1,0:T(1,128)S(1)}, u32[]{:S(2)}, u32[]{:S(2)}) async-start(f32[128,1,512]{2,1,0:T(1,128)} %reshape.483), calls=%async_computation | async-start | bytes 524288 | tf_op jit(solution)/shard_map/all_to_all | solution.py:123
  60.5 10.1 %while.60 = (s32[]{:T(128)}, f32[4,8,64]{2,1,0:T(8,128)S(1)}, s32[4,6]{0,1:T(8,128)S(1)}, s32[]{:T(128)}, f32[16,8,64]{2,1,0:T(8,128)S(1)}, /*index=5*/f32[4,3,6...) while((s32[]{:T(128)}, f32[4,8,64]{2,1,0:T(8,128)S(1)}, s32[4,6]{0,1:T(8,128)S(1)}, ...), condition=%wide.region_5.6_spmd.clone, body=%wide.region_4.5_spmd.clone.sunk | while | flops 1727519 | bytes 69875 | solution.py:48
  75.1 113.0 %while.59 = (s32[]{:T(128)}, f32[32,8,64]{2,1,0:T(8,128)S(1)}, s32[32,20]{0,1:T(8,128)}, s32[]{:T(128)}, f32[96,8,64]{2,1,0:T(8,128)S(1)}, /*index=5*/f32[32,3,6...) while((s32[]{:T(128)}, f32[32,8,64]{2,1,0:T(8,128)S(1)}, s32[32,20]{0,1:T(8,128)}, ...), condition=%wide.region_3.4_spmd.clone, body=%wide.region_2.3_spmd.clone.sunk | while | flops 13812963 | bytes 529523 | solution.py:48
  189.8 194.2 %while.58 = (s32[]{:T(128)}, f32[32,8,128]{2,1,0:T(8,128)}, s32[32,27]{0,1:T(8,128)S(1)}, s32[]{:T(128)}, f32[96,11,128]{2,1,0:T(8,128)S(1)}, /*index=5*/f32[32,3,128]{2,0,1:T(8,128)S(1)}, s32[]{:T(128)}, s32[]{:T(128)}) while((s32[]{:T(128)}, f32[32,8,128]{2,1,0:T(8,128)}, s32[32,27]{0,1:T(8,128)S(1)}, s32[]{:T(128)}, ...), condition=%wide.region_1.2_spmd.clone, body=%wide.region_0.1_spmd.clone.sunk | while | flops 55149792 | bytes 1054059 | solution.py:82
  197.1 6.5 %fusion.156 = f32[32,8,128]{2,1,0:T(8,128)} fusion(f32[32,128]{1,0:T(8,128)S(1)} %bitcast.176, f32[32,128]{1,0:T(8,128)S(1)} %get-tuple-element.912, f32[32,128]{1,0:T(8,128)S(1)} %bitcast.175, f32[32,128]{1,0:T(8,128)S(1)} %get-tuple-element.914, f32[32,128]{1,0:T(8,128)S(1)} %bitcast.174, f32[32,128]{1,0:T(8,128)S(1)} %get-tuple-element.916, ...), kind=kOutput, calls=%fused_computation.17.clone.1 | convolution fusion | flops 55148544 | bytes 492033 | tf_op jit(solution)/shard_map/while/body/eval_jaxpr/lpq,lrq->lrp/dot_general | solution.py:79
  204.3 6.5 %fusion.156 = f32[32,8,128]{2,1,0:T(8,128)} fusion(f32[32,128]{1,0:T(8,128)S(1)} %bitcast.176, f32[32,128]{1,0:T(8,128)S(1)} %get-tuple-element.912, f32[32,128]{1,0:T(8,128)S(1)} %bitcast.175, f32[32,128]{1,0:T(8,128)S(1)} %get-tuple-element.914, f32[32,128]{1,0:T(8,128)S(1)} %bitcast.174, f32[32,128]{1,0:T(8,128)S(1)} %get-tuple-element.916, ...), kind=kOutput, calls=%fused_computation.17.clone.1 | convolution fusion | flops 55148544 | bytes 492033 | tf_op jit(solution)/shard_map/while/body/eval_jaxpr/lpq,lrq->lrp/dot_general | solution.py:79
  211.5 6.5 %fusion.156 = f32[32,8,128]{2,1,0:T(8,128)} fusion(f32[32,128]{1,0:T(8,128)S(1)} %bitcast.176, f32[32,128]{1,0:T(8,128)S(1)} %get-tuple-element.912, f32[32,128]{1,0:T(8,128)S(1)} %bitcast.175, f32[32,128]{1,0:T(8,128)S(1)} %get-tuple-element.914, f32[32,128]{1,0:T(8,128)S(1)} %bitcast.174, f32[32,128]{1,0:T(8,128)S(1)} %get-tuple-element.916, ...), kind=kOutput, calls=%fused_computation.17.clone.1 | convolution fusion | flops 55148544 | bytes 492033 | tf_op jit(solution)/shard_map/while/body/eval_jaxpr/lpq,lrq->lrp/dot_general | solution.py:79
  218.7 6.5 %fusion.156 = f32[32,8,128]{2,1,0:T(8,128)} fusion(f32[32,128]{1,0:T(8,128)S(1)} %bitcast.176, f32[32,128]{1,0:T(8,128)S(1)} %get-tuple-element.912, f32[32,128]{1,0:T(8,128)S(1)} %bitcast.175, f32[32,128]{1,0:T(8,128)S(1)} %get-tuple-element.914, f32[32,128]{1,0:T(8,128)S(1)} %bitcast.174, f32[32,128]{1,0:T(8,128)S(1)} %get-tuple-element.916, ...), kind=kOutput, calls=%fused_computation.17.clone.1 | convolution fusion | flops 55148544 | bytes 492033 | tf_op jit(solution)/shard_map/while/body/eval_jaxpr/lpq,lrq->lrp/dot_general | solution.py:79
  225.9 6.5 %fusion.156 = f32[32,8,128]{2,1,0:T(8,128)} fusion(f32[32,128]{1,0:T(8,128)S(1)} %bitcast.176, f32[32,128]{1,0:T(8,128)S(1)} %get-tuple-element.912, f32[32,128]{1,0:T(8,128)S(1)} %bitcast.175, f32[32,128]{1,0:T(8,128)S(1)} %get-tuple-element.914, f32[32,128]{1,0:T(8,128)S(1)} %bitcast.174, f32[32,128]{1,0:T(8,128)S(1)} %get-tuple-element.916, ...), kind=kOutput, calls=%fused_computation.17.clone.1 | convolution fusion | flops 55148544 | bytes 492033 | tf_op jit(solution)/shard_map/while/body/eval_jaxpr/lpq,lrq->lrp/dot_general | solution.py:79
  233.2 6.5 %fusion.156 = f32[32,8,128]{2,1,0:T(8,128)} fusion(f32[32,128]{1,0:T(8,128)S(1)} %bitcast.176, f32[32,128]{1,0:T(8,128)S(1)} %get-tuple-element.912, f32[32,128]{1,0:T(8,128)S(1)} %bitcast.175, f32[32,128]{1,0:T(8,128)S(1)} %get-tuple-element.914, f32[32,128]{1,0:T(8,128)S(1)} %bitcast.174, f32[32,128]{1,0:T(8,128)S(1)} %get-tuple-element.916, ...), kind=kOutput, calls=%fused_computation.17.clone.1 | convolution fusion | flops 55148544 | bytes 492033 | tf_op jit(solution)/shard_map/while/body/eval_jaxpr/lpq,lrq->lrp/dot_general | solution.py:79
  240.4 6.5 %fusion.156 = f32[32,8,128]{2,1,0:T(8,128)} fusion(f32[32,128]{1,0:T(8,128)S(1)} %bitcast.176, f32[32,128]{1,0:T(8,128)S(1)} %get-tuple-element.912, f32[32,128]{1,0:T(8,128)S(1)} %bitcast.175, f32[32,128]{1,0:T(8,128)S(1)} %get-tuple-element.914, f32[32,128]{1,0:T(8,128)S(1)} %bitcast.174, f32[32,128]{1,0:T(8,128)S(1)} %get-tuple-element.916, ...), kind=kOutput, calls=%fused_computation.17.clone.1 | convolution fusion | flops 55148544 | bytes 492033 | tf_op jit(solution)/shard_map/while/body/eval_jaxpr/lpq,lrq->lrp/dot_general | solution.py:79
  247.6 6.5 %fusion.156 = f32[32,8,128]{2,1,0:T(8,128)} fusion(f32[32,128]{1,0:T(8,128)S(1)} %bitcast.176, f32[32,128]{1,0:T(8,128)S(1)} %get-tuple-element.912, f32[32,128]{1,0:T(8,128)S(1)} %bitcast.175, f32[32,128]{1,0:T(8,128)S(1)} %get-tuple-element.914, f32[32,128]{1,0:T(8,128)S(1)} %bitcast.174, f32[32,128]{1,0:T(8,128)S(1)} %get-tuple-element.916, ...), kind=kOutput, calls=%fused_computation.17.clone.1 | convolution fusion | flops 55148544 | bytes 492033 | tf_op jit(solution)/shard_map/while/body/eval_jaxpr/lpq,lrq->lrp/dot_general | solution.py:79
  254.8 6.5 %fusion.156 = f32[32,8,128]{2,1,0:T(8,128)} fusion(f32[32,128]{1,0:T(8,128)S(1)} %bitcast.176, f32[32,128]{1,0:T(8,128)S(1)} %get-tuple-element.912, f32[32,128]{1,0:T(8,128)S(1)} %bitcast.175, f32[32,128]{1,0:T(8,128)S(1)} %get-tuple-element.914, f32[32,128]{1,0:T(8,128)S(1)} %bitcast.174, f32[32,128]{1,0:T(8,128)S(1)} %get-tuple-element.916, ...), kind=kOutput, calls=%fused_computation.17.clone.1 | convolution fusion | flops 55148544 | bytes 492033 | tf_op jit(solution)/shard_map/while/body/eval_jaxpr/lpq,lrq->lrp/dot_general | solution.py:79
  262.0 6.5 %fusion.156 = f32[32,8,128]{2,1,0:T(8,128)} fusion(f32[32,128]{1,0:T(8,128)S(1)} %bitcast.176, f32[32,128]{1,0:T(8,128)S(1)} %get-tuple-element.912, f32[32,128]{1,0:T(8,128)S(1)} %bitcast.175, f32[32,128]{1,0:T(8,128)S(1)} %get-tuple-element.914, f32[32,128]{1,0:T(8,128)S(1)} %bitcast.174, f32[32,128]{1,0:T(8,128)S(1)} %get-tuple-element.916, ...), kind=kOutput, calls=%fused_computation.17.clone.1 | convolution fusion | flops 55148544 | bytes 492033 | tf_op jit(solution)/shard_map/while/body/eval_jaxpr/lpq,lrq->lrp/dot_general | solution.py:79
  269.2 6.5 %fusion.156 = f32[32,8,128]{2,1,0:T(8,128)} fusion(f32[32,128]{1,0:T(8,128)S(1)} %bitcast.176, f32[32,128]{1,0:T(8,128)S(1)} %get-tuple-element.912, f32[32,128]{1,0:T(8,128)S(1)} %bitcast.175, f32[32,128]{1,0:T(8,128)S(1)} %get-tuple-element.914, f32[32,128]{1,0:T(8,128)S(1)} %bitcast.174, f32[32,128]{1,0:T(8,128)S(1)} %get-tuple-element.916, ...), kind=kOutput, calls=%fused_computation.17.clone.1 | convolution fusion | flops 55148544 | bytes 492033 | tf_op jit(solution)/shard_map/while/body/eval_jaxpr/lpq,lrq->lrp/dot_general | solution.py:79
  276.5 6.5 %fusion.156 = f32[32,8,128]{2,1,0:T(8,128)} fusion(f32[32,128]{1,0:T(8,128)S(1)} %bitcast.176, f32[32,128]{1,0:T(8,128)S(1)} %get-tuple-element.912, f32[32,128]{1,0:T(8,128)S(1)} %bitcast.175, f32[32,128]{1,0:T(8,128)S(1)} %get-tuple-element.914, f32[32,128]{1,0:T(8,128)S(1)} %bitcast.174, f32[32,128]{1,0:T(8,128)S(1)} %get-tuple-element.916, ...), kind=kOutput, calls=%fused_computation.17.clone.1 | convolution fusion | flops 55148544 | bytes 492033 | tf_op jit(solution)/shard_map/while/body/eval_jaxpr/lpq,lrq->lrp/dot_general | solution.py:79
  283.7 6.5 %fusion.156 = f32[32,8,128]{2,1,0:T(8,128)} fusion(f32[32,128]{1,0:T(8,128)S(1)} %bitcast.176, f32[32,128]{1,0:T(8,128)S(1)} %get-tuple-element.912, f32[32,128]{1,0:T(8,128)S(1)} %bitcast.175, f32[32,128]{1,0:T(8,128)S(1)} %get-tuple-element.914, f32[32,128]{1,0:T(8,128)S(1)} %bitcast.174, f32[32,128]{1,0:T(8,128)S(1)} %get-tuple-element.916, ...), kind=kOutput, calls=%fused_computation.17.clone.1 | convolution fusion | flops 55148544 | bytes 492033 | tf_op jit(solution)/shard_map/while/body/eval_jaxpr/lpq,lrq->lrp/dot_general | solution.py:79
  290.9 6.5 %fusion.156 = f32[32,8,128]{2,1,0:T(8,128)} fusion(f32[32,128]{1,0:T(8,128)S(1)} %bitcast.176, f32[32,128]{1,0:T(8,128)S(1)} %get-tuple-element.912, f32[32,128]{1,0:T(8,128)S(1)} %bitcast.175, f32[32,128]{1,0:T(8,128)S(1)} %get-tuple-element.914, f32[32,128]{1,0:T(8,128)S(1)} %bitcast.174, f32[32,128]{1,0:T(8,128)S(1)} %get-tuple-element.916, ...), kind=kOutput, calls=%fused_computation.17.clone.1 | convolution fusion | flops 55148544 | bytes 492033 | tf_op jit(solution)/shard_map/while/body/eval_jaxpr/lpq,lrq->lrp/dot_general | solution.py:79
  298.1 6.5 %fusion.156 = f32[32,8,128]{2,1,0:T(8,128)} fusion(f32[32,128]{1,0:T(8,128)S(1)} %bitcast.176, f32[32,128]{1,0:T(8,128)S(1)} %get-tuple-element.912, f32[32,128]{1,0:T(8,128)S(1)} %bitcast.175, f32[32,128]{1,0:T(8,128)S(1)} %get-tuple-element.914, f32[32,128]{1,0:T(8,128)S(1)} %bitcast.174, f32[32,128]{1,0:T(8,128)S(1)} %get-tuple-element.916, ...), kind=kOutput, calls=%fused_computation.17.clone.1 | convolution fusion | flops 55148544 | bytes 492033 | tf_op jit(solution)/shard_map/while/body/eval_jaxpr/lpq,lrq->lrp/dot_general | solution.py:79
  305.3 6.5 %fusion.156 = f32[32,8,128]{2,1,0:T(8,128)} fusion(f32[32,128]{1,0:T(8,128)S(1)} %bitcast.176, f32[32,128]{1,0:T(8,128)S(1)} %get-tuple-element.912, f32[32,128]{1,0:T(8,128)S(1)} %bitcast.175, f32[32,128]{1,0:T(8,128)S(1)} %get-tuple-element.914, f32[32,128]{1,0:T(8,128)S(1)} %bitcast.174, f32[32,128]{1,0:T(8,128)S(1)} %get-tuple-element.916, ...), kind=kOutput, calls=%fused_computation.17.clone.1 | convolution fusion | flops 55148544 | bytes 492033 | tf_op jit(solution)/shard_map/while/body/eval_jaxpr/lpq,lrq->lrp/dot_general | solution.py:79
  312.6 6.5 %fusion.156 = f32[32,8,128]{2,1,0:T(8,128)} fusion(f32[32,128]{1,0:T(8,128)S(1)} %bitcast.176, f32[32,128]{1,0:T(8,128)S(1)} %get-tuple-element.912, f32[32,128]{1,0:T(8,128)S(1)} %bitcast.175, f32[32,128]{1,0:T(8,128)S(1)} %get-tuple-element.914, f32[32,128]{1,0:T(8,128)S(1)} %bitcast.174, f32[32,128]{1,0:T(8,128)S(1)} %get-tuple-element.916, ...), kind=kOutput, calls=%fused_computation.17.clone.1 | convolution fusion | flops 55148544 | bytes 492033 | tf_op jit(solution)/shard_map/while/body/eval_jaxpr/lpq,lrq->lrp/dot_general | solution.py:79
  319.8 6.5 %fusion.156 = f32[32,8,128]{2,1,0:T(8,128)} fusion(f32[32,128]{1,0:T(8,128)S(1)} %bitcast.176, f32[32,128]{1,0:T(8,128)S(1)} %get-tuple-element.912, f32[32,128]{1,0:T(8,128)S(1)} %bitcast.175, f32[32,128]{1,0:T(8,128)S(1)} %get-tuple-element.914, f32[32,128]{1,0:T(8,128)S(1)} %bitcast.174, f32[32,128]{1,0:T(8,128)S(1)} %get-tuple-element.916, ...), kind=kOutput, calls=%fused_computation.17.clone.1 | convolution fusion | flops 55148544 | bytes 492033 | tf_op jit(solution)/shard_map/while/body/eval_jaxpr/lpq,lrq->lrp/dot_general | solution.py:79
  348.6 6.5 %fusion.156 = f32[32,8,128]{2,1,0:T(8,128)} fusion(f32[32,128]{1,0:T(8,128)S(1)} %bitcast.176, f32[32,128]{1,0:T(8,128)S(1)} %get-tuple-element.912, f32[32,128]{1,0:T(8,128)S(1)} %bitcast.175, f32[32,128]{1,0:T(8,128)S(1)} %get-tuple-element.914, f32[32,128]{1,0:T(8,128)S(1)} %bitcast.174, f32[32,128]{1,0:T(8,128)S(1)} %get-tuple-element.916, ...), kind=kOutput, calls=%fused_computation.17.clone.1 | convolution fusion | flops 55148544 | bytes 492033 | tf_op jit(solution)/shard_map/while/body/eval_jaxpr/lpq,lrq->lrp/dot_general | solution.py:79
  386.0 13.1 %while.61 = (s32[]{:T(128)}, f32[1,8,64]{2,1,0:T(8,128)S(1)}, s32[1,6]{1,0:T(1,128)S(1)}, f32[128,8,64]{2,1,0:T(8,128)S(1)}, f32[1,3,64]{2,1,0:T(4,128)S(1)}, /*...) while((s32[]{:T(128)}, f32[1,8,64]{2,1,0:T(8,128)S(1)}, ...), condition=%wide.region_8.9_spmd.clone, body=%wide.region_7.8_spmd.clone.sunk | while | flops 431623 | bytes 18109 | solution.py:48
  (489 shorter events, 245.7 us)
Async XLA Ops:
  0.0 22.0 %copy-start = (f32[32,64,64]{2,1,0:T(8,128)S(1)}, f32[32,64,64]{2,1,0:T(8,128)}, u32[]{:S(2)}) copy-start(f32[32,64,64]{2,1,0:T(8,128)} %param.24) | copy-start | bytes 1572868
  2.4 3.5 copy-start.12
  2.4 14.4 %copy-start.2 = (f32[32,3,128]{2,0,1:T(8,128)S(1)}, f32[32,3,128]{2,0,1:T(8,128)}, u32[]{:S(2)}) copy-start(f32[32,3,128]{2,0,1:T(8,128)} %param.19) | copy-start | bytes 147460
  2.4 14.5 %copy-start.3 = (f32[32,8,128]{2,1,0:T(8,128)S(1)}, f32[32,8,128]{2,1,0:T(8,128)}, u32[]{:S(2)}) copy-start(f32[32,8,128]{2,1,0:T(8,128)} %param.20) | copy-start | bytes 393220
  5.9 16.7 %copy-start.4 = (f32[4,64,64]{2,1,0:T(8,128)S(1)}, f32[4,64,64]{2,1,0:T(8,128)}, u32[]{:S(2)}) copy-start(f32[4,64,64]{2,1,0:T(8,128)} %param.25) | copy-start | bytes 196612
  6.0 65.5 %collective-permute-start.2 = (f32[32,11,64]{2,1,0:T(8,128)S(1)}, f32[32,11,64]{2,1,0:T(8,128)}, u32[]{:S(2)}, u32[]{:S(2)}) collective-permute-start(f32[32,11,64]{2,1,0:T(8,128)S(1)} %pad_maximum_fusion.3), channel_id=1, source_target_pairs={{0,1},{1,2},{2,3},{3,4},{4,5},{5,6},{6,7},{7,8},{8,9},{9,10},{10,1... | collective-permute-start | bytes 270344 | tf_op jit(solution)/shard_map/ppermute | solution.py:16
  10.6 62.0 %collective-permute-start.3 = (f32[32,11,64]{2,1,0:T(8,128)S(1)}, f32[32,11,64]{2,1,0:T(8,128)}, u32[]{:S(2)}, u32[]{:S(2)}) collective-permute-start(f32[32,11,64]{2,1,0:T(8,128)S(1)} %pad_maximum_fusion.3), channel_id=1, source_target_pairs={{1,0},{2,1},{3,2},{4,3},{5,4},{6,5},{7,6},{8,7},{9,8},{10,9},{11,1... | collective-permute-start | bytes 270344 | tf_op jit(solution)/shard_map/ppermute | solution.py:19
  17.0 171.1 %collective-permute-start = (f32[32,11,128]{2,1,0:T(8,128)S(1)}, f32[32,11,128]{2,1,0:T(8,128)}, u32[]{:S(2)}, u32[]{:S(2)}) collective-permute-start(f32[32,11,128]{2,1,0:T(8,128)S(1)} %pad_maximum_fusion.2), channel_id=1, source_target_pairs={{0,1},{1,2},{2,3},{3,4},{4,5},{5,6},{6,7},{7,8},{8,9},{9,10},{10,1... | collective-permute-start | bytes 540680 | tf_op jit(solution)/shard_map/ppermute | solution.py:16
  18.9 169.8 %collective-permute-start.1 = (f32[32,11,128]{2,1,0:T(8,128)S(1)}, f32[32,11,128]{2,1,0:T(8,128)}, u32[]{:S(2)}, u32[]{:S(2)}) collective-permute-start(f32[32,11,128]{2,1,0:T(8,128)S(1)} %pad_maximum_fusion.2), channel_id=1, source_target_pairs={{1,0},{2,1},{3,2},{4,3},{5,4},{6,5},{7,6},{8,7},{9,8},{10,9},{11,1... | collective-permute-start | bytes 540680 | tf_op jit(solution)/shard_map/ppermute | solution.py:19
  28.1 26.0 %copy-start.5 = (f32[4,3,64]{2,0,1:T(4,128)S(1)}, f32[4,3,64]{2,0,1:T(4,128)}, u32[]{:S(2)}) copy-start(f32[4,3,64]{2,0,1:T(4,128)} %param.22) | copy-start | bytes 9220
  28.1 32.4 %copy-start.17 = (s32[4,6]{1,0:T(4,128)S(1)}, s32[4,6]{1,0:T(4,128)}, u32[]{:S(2)}) copy-start(s32[4,6]{1,0:T(4,128)} %param.28) | copy-start | bytes 292
  29.1 354.9 %all-to-all-start = ((f32[128,1,512]{2,1,0:T(1,128)}), f32[128,1,512]{2,1,0:T(1,128)S(1)}, u32[]{:S(2)}, u32[]{:S(2)}) async-start(f32[128,1,512]{2,1,0:T(1,128)} %reshape.483), calls=%async_computation | async-start | bytes 524288 | tf_op jit(solution)/shard_map/all_to_all | solution.py:123
  60.5 10.7 %copy-start.10 = (f32[128,3,64]{0,2,1:T(8,128)S(1)}, f32[128,3,64]{0,2,1:T(8,128)}, u32[]{:S(2)}) copy-start(f32[128,3,64]{0,2,1:T(8,128)} %param.23) | copy-start | bytes 294916
  60.5 10.8 %copy-start.11 = (s32[32,27]{1,0:T(8,128)S(1)}, s32[32,27]{1,0:T(8,128)}, u32[]{:S(2)}) copy-start(s32[32,27]{1,0:T(8,128)} %param.26) | copy-start | bytes 10372
  70.6 0.6 copy-start.14
  74.0 0.8 copy-start.1
  74.1 0.9 copy-start.7
  188.1 0.7 copy-start.8
  384.0 2.0 copy-start.16
  385.9 13.3 %copy-start.15 = (f32[4,8,64]{2,1,0:T(8,128)S(1)}, f32[4,8,64]{2,1,0:T(8,128)}, u32[]{:S(2)}) copy-start(f32[4,8,64]{2,1,0:T(8,128)} %copy-done.14) | copy-start | bytes 24580
  386.0 16.1 %copy-start.9 = (f32[32,8,64]{2,1,0:T(8,128)S(1)}, f32[32,8,64]{2,1,0:T(8,128)}, u32[]{:S(2)}) copy-start(f32[32,8,64]{2,1,0:T(8,128)} %copy-done.8) | copy-start | bytes 196612
  399.2 3.0 copy-start.13
  402.2 1.9 copy-start.6
